TPU v7x, 32 devices: a whole 2x2x4 slice. The times are simulated.
32 devices in a mesh: pair: 8 (over z, y), chan: 4 (over x, core).
Axes of the slice: x: 2, y: 2, z: 4, core: 2. Of those that a mesh axis runs over, the one named last changes fastest.
Arguments:
- jones_init: float32 [512, 4, 128], P('pair', 'chan'), may hold values from -2 to 2
- dual_init: float32 [512, 4, 128], P('pair', 'chan'), may hold values from -1.2 to 1.2
- penalty: float32 [16], replicated, may hold values from 0.5 to 5
- sky_flux: float32 [4, 4, 16], P('chan'), may hold values from -0.1 to 0.5, as said below
- visibility: bfloat16 [8, 4, 8, 2, 128, 128], P('pair', 'chan'), may hold values from -4 to 4
- phases: float32 [8, 8, 2, 1024], P('pair'), may hold values from -3.1416 to 3.1416, as said below
- pair_ids: int32 [8], P('pair'), may hold values from 0 to 35, as said below
- counts: int32 [8], P('pair'), may hold values from 2 to 8, as said below
- slot_flags: int32 [8, 8], P('pair'), may hold values 0 or 1
Outputs:
- jones_final: float32 [512, 4, 128], P('pair', 'chan')
- duals_final: float32 [512, 4, 128], P('pair', 'chan')
- consensus: float32 [512, 3, 128], P('pair')
Inputs may be any that keep to these rules, and one draw needn't show every extreme that they name: `sky_flux`: [f, 0, k] and [f, 1, k] are the two polarized fluxes, [f, 2, k] and [f, 3, k] the real and imaginary cross terms. `phases`: [t, s, 0, k * 64 + p] is the phase of direction k at row station p in slot s, [t, s, 1, ...] that at column station p, before scaling by frequency. `pair_ids`: block pair of each tile, numbered row by row over blocks a <= b of 8. A tile keeps slots 0 to counts - 1; tiles whose column block lies 8 // 2 or more blocks after their row block keep all 8.
All inputs are finite; a program needn't handle non-finite values. No bound on the sum of `slot_flags` on one device may be relied on, other than what follows from the above.
Results may differ from a plain program's by a relative error of at most 0.00076.
Values sent between devices are 32-bit elements; how exact they have to be, the bound alone decides.
A program may use at most 64 MiB of HBM per device.

v0:
```python
import jax
import jax.numpy as jnp
import numpy as np
from jax import lax
from jax.sharding import PartitionSpec as P

STATIONS = 512
DIRS = 16
BLOCK = 64
TIME = 8
NPOLY = 3
ITERS = 2


STEP_SCALE = 0.3
FULL_PRECISION = lax.Precision.HIGHEST


def pair_tables(block_count):
    row_list = []
    col_list = []
    for row_block in range(block_count):
        for col_block in range(row_block, block_count):
            row_list.append(row_block)
            col_list.append(col_block)
    return (np.array(row_list, np.int32), np.array(col_list, np.int32))


def split_parts(block_jones):
    station_count = block_jones.shape[0]
    chan_count = block_jones.shape[1]
    shaped = block_jones.reshape(station_count, chan_count, 2, 2, 2, DIRS)
    shaped = jnp.transpose(shaped, (2, 1, 0, 3, 5, 4))
    return (shaped[0], shaped[1])


def sky_parts(sky_flux):
    flux_xx = sky_flux[:, 0]
    flux_yy = sky_flux[:, 1]
    cross_re = sky_flux[:, 2]
    cross_im = sky_flux[:, 3]
    zeros_k = jnp.zeros_like(flux_xx)
    real_part = jnp.stack(
        [jnp.stack([flux_xx, cross_re], -1), jnp.stack([cross_re, flux_yy], -1)], -2
    )
    imag_part = jnp.stack(
        [jnp.stack([zeros_k, cross_im], -1), jnp.stack([-cross_im, zeros_k], -1)], -2
    )
    return (real_part, imag_part)


def times_sky(parts, sky_pair):
    jones_re = parts[0][..., None]
    jones_im = parts[1][..., None]
    sky_re = sky_pair[0][:, None, None]
    sky_im = sky_pair[1][:, None, None]
    out_re = jnp.sum(jones_re * sky_re - jones_im * sky_im, axis=-2)
    out_im = jnp.sum(jones_re * sky_im + jones_im * sky_re, axis=-2)
    return (out_re, out_im)


def phase_angles(theta_side, freq_ratio):
    slot_count = theta_side.shape[0]
    shaped = jnp.transpose(theta_side.reshape(slot_count, DIRS, BLOCK), (0, 2, 1))
    angle_all = freq_ratio[:, None, None, None] * shaped[None]
    angle_all = angle_all[:, :, :, None, :, None]
    return (jnp.cos(angle_all), jnp.sin(angle_all))


def rotate_flat(parts, cosines, sines):
    part_re = parts[0][:, None]
    part_im = parts[1][:, None]
    out_re = cosines * part_re - sines * part_im
    out_im = cosines * part_im + sines * part_re
    chan_count = out_re.shape[0]
    slot_count = out_re.shape[1]
    return (
        out_re.reshape(chan_count, slot_count, 2 * BLOCK, 2 * DIRS).astype(jnp.bfloat16),
        out_im.reshape(chan_count, slot_count, 2 * BLOCK, 2 * DIRS).astype(jnp.bfloat16),
    )


def unrotate(product, cosines, sines):
    chan_count = product.shape[0]
    slot_count = product.shape[1]
    shaped = product.reshape(chan_count, slot_count, BLOCK, 2, 2, DIRS, 2)
    neg_re = shaped[:, :, :, :, 0]
    neg_im = shaped[:, :, :, :, 1]
    grad_re = -jnp.sum(neg_re * cosines + neg_im * sines, axis=1)
    grad_im = -jnp.sum(neg_im * cosines - neg_re * sines, axis=1)
    both_parts = jnp.transpose(jnp.stack([grad_re, grad_im], 0), (2, 1, 0, 3, 5, 4))
    return both_parts.reshape(BLOCK, chan_count, 8 * DIRS)


def power_rows(parts):
    power = jnp.sum(parts[0] * parts[0] + parts[1] * parts[1], axis=2)
    power = jnp.transpose(power, (1, 0, 3, 2))
    return power.reshape(power.shape[0], -1)


def slot_terms(vis_part, weights, theta_part, freq_ratio, row_sky, col_sky, col_parts, mask_wide):
    cos_row, sin_row = phase_angles(theta_part[:, 0], freq_ratio)
    cos_col, sin_col = phase_angles(theta_part[:, 1], freq_ratio)
    left_re, left_im = rotate_flat(row_sky, cos_row, sin_row)
    right_re, right_im = rotate_flat(col_sky, cos_col, sin_col)
    conj_re, conj_im = rotate_flat(col_parts, cos_col, sin_col)
    left_side = jnp.concatenate([left_re, left_im], -1)
    model_rhs = jnp.stack(
        [jnp.concatenate([conj_re, conj_im], -1), jnp.concatenate([-conj_im, conj_re], -1)], 2
    )
    predicted = jnp.einsum(
        "ftpk,ftcqk->ftcpq", left_side, model_rhs, preferred_element_type=jnp.float32
    )
    weighting = weights[None, :, None, None, None] * mask_wide
    residual = (weighting * (vis_part.astype(jnp.float32) - predicted)).astype(jnp.bfloat16)
    row_rhs = jnp.stack(
        [jnp.concatenate([right_re, right_im], -1), jnp.concatenate([-right_im, right_re], -1)], 2
    )
    col_rhs = jnp.stack(
        [jnp.concatenate([left_re, left_im], -1), jnp.concatenate([left_im, -left_re], -1)], 2
    )
    row_out = jnp.einsum("ftcpq,ftcqk->ftpk", residual, row_rhs, preferred_element_type=jnp.float32)
    col_out = jnp.einsum("ftcpq,ftcpk->ftqk", residual, col_rhs, preferred_element_type=jnp.float32)
    return (unrotate(row_out, cos_row, sin_row), unrotate(col_out, cos_col, sin_col))


def tile_terms(
    full_jones, sky_pair, freq_ratio, tables, vis_tile, theta_tile, pair_id, kept_slots, flag_row
):
    pair_range = jnp.arange(tables[0].shape[0])
    row_block = jnp.sum(jnp.where(pair_range == pair_id, tables[0], 0)).astype(jnp.int32)
    col_block = jnp.sum(jnp.where(pair_range == pair_id, tables[1], 0)).astype(jnp.int32)
    row_jones = lax.dynamic_slice_in_dim(full_jones, row_block * BLOCK, BLOCK, 0)
    col_jones = lax.dynamic_slice_in_dim(full_jones, col_block * BLOCK, BLOCK, 0)
    row_sky = times_sky(split_parts(row_jones), sky_pair)
    col_parts = split_parts(col_jones)
    col_sky = times_sky(col_parts, sky_pair)
    station_rank = jnp.arange(BLOCK)
    strict = (station_rank[:, None] < station_rank[None, :]) | (row_block != col_block)
    pair_mask = strict.astype(jnp.float32)
    mask_wide = jnp.broadcast_to(pair_mask[:, None, :, None], (BLOCK, 2, BLOCK, 2)).reshape(
        2 * BLOCK, 2 * BLOCK
    )
    weights = flag_row.astype(jnp.float32) * (jnp.arange(TIME) < kept_slots).astype(jnp.float32)
    samples = jnp.sum(weights)
    chan_count = full_jones.shape[1]
    row_grad, col_grad = slot_terms(
        vis_tile, weights, theta_tile, freq_ratio, row_sky, col_sky, col_parts, mask_wide
    )
    row_curv = samples * jnp.dot(pair_mask, power_rows(col_sky), precision=FULL_PRECISION)
    col_curv = samples * jnp.dot(pair_mask.T, power_rows(row_sky), precision=FULL_PRECISION)
    return (
        row_block,
        col_block,
        row_grad,
        col_grad,
        row_curv.reshape(BLOCK, chan_count, 2 * DIRS),
        col_curv.reshape(BLOCK, chan_count, 2 * DIRS),
    )


def add_block(total, start, piece):
    current = lax.dynamic_slice_in_dim(total, start, piece.shape[0], 0)
    return lax.dynamic_update_slice_in_dim(total, current + piece, start, 0)


def data_terms(
    full_jones, sky_pair, freq_ratio, tables, visibility, phases, pair_ids, counts, slot_flags
):
    station_count = full_jones.shape[0]
    chan_count = full_jones.shape[1]
    grad_zero = jnp.zeros((station_count, chan_count, 8 * DIRS), jnp.float32)
    curv_zero = jnp.zeros((station_count, chan_count, 2 * DIRS), jnp.float32)

    def add_tile(carry, tile_inputs):
        grad_sum, curv_sum = carry
        vis_tile, theta_tile, pair_id, kept_slots, flag_row = tile_inputs
        row_block, col_block, row_grad, col_grad, row_curv, col_curv = tile_terms(
            full_jones,
            sky_pair,
            freq_ratio,
            tables,
            vis_tile,
            theta_tile,
            pair_id,
            kept_slots,
            flag_row,
        )
        grad_sum = add_block(grad_sum, row_block * BLOCK, row_grad)
        grad_sum = add_block(grad_sum, col_block * BLOCK, col_grad)
        curv_sum = add_block(curv_sum, row_block * BLOCK, row_curv)
        curv_sum = add_block(curv_sum, col_block * BLOCK, col_curv)
        return ((grad_sum, curv_sum), None)

    totals, unused = lax.scan(
        add_tile, (grad_zero, curv_zero), (visibility, phases, pair_ids, counts, slot_flags)
    )
    return totals


def cosine_basis(chan_total):
    middle = jnp.arange(chan_total, dtype=jnp.float32) + 0.5
    degree = jnp.arange(NPOLY, dtype=jnp.float32)
    normalizer = jnp.sqrt(jnp.where(degree == 0, 1.0, 2.0) / chan_total)
    return jnp.cos(jnp.pi * middle[:, None] * degree[None, :] / chan_total) * normalizer[None, :]


def project(values_all, poly_basis):
    return jnp.sum(poly_basis[None, :, :, None] * values_all[:, :, None, :], axis=1)


def expand(coefficients, poly_basis):
    return jnp.sum(poly_basis[None, :, :, None] * coefficients[:, None, :, :], axis=2)


def jacobi(jones_now, duals_now, gradient, curvature, penalty_full, target):
    divisor = jnp.tile(curvature, (1, 1, 4)) + 0.5 * penalty_full
    return (
        jones_now
        - STEP_SCALE
        * (gradient + 0.5 * penalty_full * (jones_now - target) + 0.5 * duals_now)
        / divisor
    )


def per_device(
    jones_init, dual_init, penalty, sky_flux, visibility, phases, pair_ids, counts, slot_flags
):
    chan_dev = jones_init.shape[1]
    chan_total = chan_dev * lax.axis_size("chan")
    chan_start = lax.axis_index("chan") * chan_dev
    freq_ratio = 1.0 + (chan_start + jnp.arange(chan_dev)).astype(jnp.float32) / chan_total
    poly_basis = lax.dynamic_slice_in_dim(cosine_basis(chan_total), chan_start, chan_dev, 0)
    penalty_full = jnp.tile(penalty, 8)
    sky_pair = sky_parts(sky_flux)
    row_table, col_table = pair_tables(STATIONS // BLOCK)
    tables = (jnp.asarray(row_table), jnp.asarray(col_table))

    def every_consensus(current, dual_now):
        return lax.psum(project(current + dual_now / penalty_full, poly_basis), "chan")

    jones_now, duals_now = (
        lax.all_gather(jones_init, "pair", axis=0, tiled=True),
        lax.all_gather(dual_init, "pair", axis=0, tiled=True),
    )
    center = every_consensus(jones_now, duals_now)
    for outer_round in range(ITERS):
        target = expand(center, poly_basis)
        grad_full, curv_full = data_terms(
            jones_now,
            sky_pair,
            freq_ratio,
            tables,
            visibility,
            phases,
            pair_ids,
            counts,
            slot_flags,
        )
        gradient, curvature = lax.psum((grad_full, curv_full), "pair")
        jones_now = jacobi(jones_now, duals_now, gradient, curvature, penalty_full, target)
        center = every_consensus(jones_now, duals_now)
        duals_now = duals_now + penalty_full * (jones_now - expand(center, poly_basis))
    own_rows = jones_init.shape[0]
    own_start = lax.axis_index("pair") * own_rows
    return (
        lax.dynamic_slice_in_dim(jones_now, own_start, own_rows, 0),
        lax.dynamic_slice_in_dim(duals_now, own_start, own_rows, 0),
        lax.dynamic_slice_in_dim(center, own_start, own_rows, 0),
    )


def solution(mesh):
    in_specs = (
        P("pair", "chan", None),
        P("pair", "chan", None),
        P(),
        P("chan", None, None),
        P("pair", "chan", None, None, None, None),
        P("pair", None, None, None),
        P("pair"),
        P("pair"),
        P("pair", None),
    )
    out_specs = (P("pair", "chan", None), P("pair", "chan", None), P("pair", None, None))
    return jax.shard_map(
        per_device, mesh=mesh, in_specs=in_specs, out_specs=out_specs, check_vma=False
    )
```

profile of v0, /device:TPU:0, one launch (start us, length us, event | category | flops | bytes accessed | tf_op | source)
XLA Modules:
  0.0 485.5 jit_solution(17189194167199863357)
XLA Ops:
  11.9 32.8 %all_gather.6 = f32[512,1,128]{2,1,0:T(1,128)S(1)} all-gather(f32[64,1,128]{2,1,0:T(1,128)} %param.11), channel_id=1, replica_groups=mesh['pair'=8,'chan'=4] {'pair'}, dimensions={0}, use_global_device_ids=true | all-gather | bytes 294912 | tf_op jit(solution)/shard_map/all_gather | solution.py:243
  47.9 2.9 cosine_reduce_fusion
  61.6 2.4 mul.1652
  64.0 2.7 copy.299
  67.1 2.4 mul.1658
  69.6 2.7 copy.302
  75.6 2.5 broadcast_in_dim.77
  78.1 4.2 mul.1646
  88.8 4.4 copy.330
  93.2 7.2 %add_reduce_fusion.2 = (f32[64,2,16,2]{3,2,1,0:T(8,128)S(1)}, f32[64,2,16,2]{3,2,1,0:T(8,128)}) fusion(f32[1,8,64,2,2,16,2]{1,6,5,4,3,2,0:T(2,128)} %bitcast.414, f32[8,64,16]{0,2,1:T(8,128)S(1)} %bitcast.426, f32[8,64,16]{0,2,1:T(8,128)S(1)} %bitcast.423), kind=kLoop, calls=%fused_computation.13 | loop fusion | flops 253952 | bytes 360448 | tf_op jit(solution)/shard_map/while/body/eval_jaxpr/reduce_sum | solution.py:89
  101.4 2.4 copy.332
  103.9 2.3 negate_bitcast_fusion.4
  106.2 2.4 copy.333
  111.3 4.4 copy.323
  115.7 7.6 %add_reduce_fusion.3 = (f32[64,2,16,2]{3,2,1,0:T(8,128)S(1)}, f32[64,2,16,2]{3,2,1,0:T(8,128)}) fusion(f32[1,8,64,2,2,16,2]{1,6,5,4,3,2,0:T(2,128)} %bitcast.415, f32[8,64,16]{0,2,1:T(8,128)S(1)} %bitcast.420, f32[8,64,16]{0,2,1:T(8,128)S(1)} %bitcast.417), kind=kLoop, calls=%fused_computation.15 | loop fusion | flops 253952 | bytes 360448 | tf_op jit(solution)/shard_map/while/body/eval_jaxpr/reduce_sum | solution.py:89
  124.4 1.8 copy.325
  126.2 2.3 negate_bitcast_fusion.6
  128.5 1.8 copy.326
  136.1 2.1 fusion.13
  140.4 31.0 %all_gather.7 = f32[512,1,128]{2,1,0:T(1,128)S(1)} all-gather(f32[64,1,128]{2,1,0:T(1,128)} %param.12), channel_id=1, replica_groups=mesh['pair'=8,'chan'=4] {'pair'}, dimensions={0}, use_global_device_ids=true | all-gather | bytes 294912 | tf_op jit(solution)/shard_map/all_gather | solution.py:244
  174.2 38.4 %all-reduce.18.cloned.1.call-done = (f32[512,1,128]{2,0,1:T(8,128)}, f32[512,32]{0,1:T(8,128)}) async-done(((f32[512,1,128]{2,0,1:T(8,128)}, f32[512,32]{0,1:T(8,128)}), (f32[512,1,128]{2,0,1:T(8,128)}, f32[512,32]{0,1:T(8,128)})) %all-reduce.18.cloned.1.call-update) | async-done | bytes 327696 | tf_op jit(solution)/shard_map/psum | solution.py:260
  212.7 1.6 tile.34
  214.2 1.8 copy.343
  216.0 33.2 %all-reduce.10.cloned.1.call-done = f32[512,3,128]{2,0,1:T(8,128)} async-done(((f32[512,3,128]{2,0,1:T(8,128)}), f32[512,3,128]{2,0,1:T(8,128)}) %all-reduce.10.cloned.1.call-update) | async-done | bytes 786448 | tf_op jit(solution)/shard_map/psum | solution.py:240
  250.5 1.9 add_bitcast_fusion.1
  260.6 2.1 copy.354
  262.7 1.7 mul.1758
  264.4 2.1 copy.356
  266.5 2.3 mul.1763
  268.8 1.7 fusion.58
  270.5 1.6 add_convert_fusion.1
  272.1 2.1 copy.360
  274.2 1.7 mul.1775
  275.9 2.1 copy.362
  278.1 2.3 mul.1780
  280.4 2.1 copy.346
  282.5 2.3 mul.1744
  284.8 2.1 copy.348
  286.9 2.3 mul.1747
  289.2 1.6 subtract_convert_fusion
  290.9 1.6 fusion.59
  297.1 4.6 copy.376
  301.7 6.2 %add_reduce_fusion = (f32[64,2,16,2]{3,2,1,0:T(8,128)S(1)}, f32[64,2,16,2]{3,2,1,0:T(8,128)S(1)}) fusion(f32[1,8,64,2,2,16,2]{1,6,5,4,3,2,0:T(2,128)} %bitcast.412, f32[8,64,16]{0,2,1:T(8,128)S(1)} %bitcast.427, f32[8,64,16]{0,2,1:T(8,128)S(1)} %bitcast.424), kind=kLoop, calls=%fused_computation.9 | loop fusion | flops 253952 | bytes 360448 | tf_op jit(solution)/shard_map/while/body/eval_jaxpr/reduce_sum | solution.py:89
  313.0 4.4 copy.368
  317.4 6.2 %add_reduce_fusion.1 = (f32[64,2,16,2]{3,2,1,0:T(8,128)S(1)}, f32[64,2,16,2]{3,2,1,0:T(8,128)S(1)}) fusion(f32[1,8,64,2,2,16,2]{1,6,5,4,3,2,0:T(2,128)} %bitcast.413, f32[8,64,16]{0,2,1:T(8,128)S(1)} %bitcast.421, f32[8,64,16]{0,2,1:T(8,128)S(1)} %bitcast.418), kind=kLoop, calls=%fused_computation.11 | loop fusion | flops 253952 | bytes 360448 | tf_op jit(solution)/shard_map/while/body/eval_jaxpr/reduce_sum | solution.py:89
  329.4 70.8 %all-reduce.16.cloned.1.call-done = (f32[512,32]{0,1:T(8,128)}, f32[512,1,128]{2,0,1:T(8,128)}) async-done(((f32[512,32]{0,1:T(8,128)}, f32[512,1,128]{2,0,1:T(8,128)}), (f32[512,32]{0,1:T(8,128)}, f32[512,1,128]{2,0,1:T(8,128)})) %all-reduce.16.cloned.1.call-update) | async-done | bytes 327696 | tf_op jit(solution)/shard_map/psum | solution.py:260
  401.2 35.5 %all-reduce.12.cloned.1.call-done = f32[512,3,128]{2,0,1:T(8,128)} async-done(((f32[512,3,128]{2,0,1:T(8,128)}), f32[512,3,128]{2,0,1:T(8,128)}) %all-reduce.12.cloned.1.call-update) | async-done | bytes 786448 | tf_op jit(solution)/shard_map/psum | solution.py:240
  440.2 35.2 %all-reduce.14.cloned.1.call-done = f32[512,3,128]{2,0,1:T(8,128)} async-done(((f32[512,3,128]{2,0,1:T(8,128)}), f32[512,3,128]{2,0,1:T(8,128)}) %all-reduce.14.cloned.1.call-update) | async-done | bytes 786448 | tf_op jit(solution)/shard_map/psum | solution.py:240
  (230 shorter events, 73.0 us)
Async XLA Ops:
  7.2 205.5 %all-reduce.18.cloned.1.call-start = ((), (), s32[]{:S(2)}) async-start(), calls=%async_computation.4 | async-start | bytes 655360 | tf_op jit(solution)/shard_map/psum | solution.py:260
  44.6 1.0 copy-start.3
  46.1 1.8 copy-start.17
  46.1 1.8 copy-start.19
  46.1 11.5 %copy-start.21 = (f32[64,2,16,2]{0,2,3,1:T(8,128)}, f32[64,2,16,2]{0,2,3,1:T(8,128)S(1)}, u32[]{:S(2)}) copy-start(f32[64,2,16,2]{0,2,3,1:T(8,128)S(1)} %get-tuple-element.97) | copy-start | bytes 49156
  46.1 12.4 %copy-start.23 = (f32[64,2,16,2]{0,2,3,1:T(8,128)}, f32[64,2,16,2]{0,2,3,1:T(8,128)S(1)}, u32[]{:S(2)}) copy-start(f32[64,2,16,2]{0,2,3,1:T(8,128)S(1)} %get-tuple-element.112) | copy-start | bytes 49156
  46.1 1.8 copy-start.34
  53.6 3.5 copy-start.1
  56.3 3.1 copy-start.2
  57.7 1.8 copy-start.31
  59.5 1.8 copy-start.33
  61.6 5.1 %copy-start.32 = (f32[8,1024]{1,0:T(8,128)S(1)}, f32[8,1024]{1,0:T(8,128)}, u32[]{:S(2)}) copy-start(f32[8,1024]{1,0:T(8,128)} %get-tuple-element.117) | copy-start | bytes 98308
  69.6 5.3 %copy-start.22 = (f32[64,2,16,2]{0,2,3,1:T(8,128)S(1)}, f32[64,2,16,2]{0,2,3,1:T(8,128)}, u32[]{:S(2)}) copy-start(f32[64,2,16,2]{0,2,3,1:T(8,128)} %copy-done.21) | copy-start | bytes 49156
  69.6 5.4 %copy-start.24 = (f32[64,2,16,2]{0,2,3,1:T(8,128)S(1)}, f32[64,2,16,2]{0,2,3,1:T(8,128)}, u32[]{:S(2)}) copy-start(f32[64,2,16,2]{0,2,3,1:T(8,128)} %copy-done.23) | copy-start | bytes 49156
  69.6 6.0 %copy-start.18 = (f32[64,2,16,2]{0,2,3,1:T(8,128)S(1)}, f32[64,2,16,2]{0,2,3,1:T(8,128)}, u32[]{:S(2)}) copy-start(f32[64,2,16,2]{0,2,3,1:T(8,128)} %copy-done.17) | copy-start | bytes 49156
  69.6 6.0 %copy-start.20 = (f32[64,2,16,2]{0,2,3,1:T(8,128)S(1)}, f32[64,2,16,2]{0,2,3,1:T(8,128)}, u32[]{:S(2)}) copy-start(f32[64,2,16,2]{0,2,3,1:T(8,128)} %copy-done.19) | copy-start | bytes 49156
  72.3 5.8 %copy-start = (f32[1,8,128,32]{2,3,1,0:T(8,128)}, f32[1,8,128,32]{2,3,1,0:T(8,128)S(1)}, u32[]{:S(2)}) copy-start(f32[1,8,128,32]{2,3,1,0:T(8,128)S(1)} %copy.302) | copy-start | bytes 393220
  78.1 5.6 %copy-start.15 = (bf16[1,1,8,2,128,128]{5,4,3,2,1,0:T(8,128)(2,1)S(1)}, bf16[1,1,8,2,128,128]{5,4,3,2,1,0:T(8,128)(2,1)}, u32[]{:S(2)}) copy-start(bf16[1,1,8,2,128,128]{5,4,3,2,1,0:T(8,128)(2,1)} %param.15) | copy-start | bytes 1572868
  78.1 8.2 %copy-start.11 = (bf16[1,8,128,32]{2,3,1,0:T(8,128)(2,1)S(1)}, bf16[1,8,128,32]{2,3,1,0:T(8,128)(2,1)}, u32[]{:S(2)}) copy-start(bf16[1,8,128,32]{2,3,1,0:T(8,128)(2,1)} %get-tuple-element.141) | copy-start | bytes 196612
  78.1 8.2 %copy-start.12 = (bf16[1,8,128,32]{2,3,1,0:T(8,128)(2,1)S(1)}, bf16[1,8,128,32]{2,3,1,0:T(8,128)(2,1)}, u32[]{:S(2)}) copy-start(bf16[1,8,128,32]{2,3,1,0:T(8,128)(2,1)} %add_convert_fusion.4) | copy-start | bytes 196612
  78.1 8.2 %copy-start.30 = (bf16[1,8,128,32]{2,3,1,0:T(8,128)(2,1)S(1)}, bf16[1,8,128,32]{2,3,1,0:T(8,128)(2,1)}, u32[]{:S(2)}) copy-start(bf16[1,8,128,32]{2,3,1,0:T(8,128)(2,1)} %get-tuple-element.140) | copy-start | bytes 196612
  87.7 0.8 copy-start.5
  101.4 8.6 %copy-start.25 = (bf16[1,8,128,32]{2,3,1,0:T(8,128)(2,1)S(1)}, bf16[1,8,128,32]{2,3,1,0:T(8,128)(2,1)}, u32[]{:S(2)}) copy-start(bf16[1,8,128,32]{2,3,1,0:T(8,128)(2,1)} %get-tuple-element.142) | copy-start | bytes 196612
  101.4 8.6 %copy-start.26 = (bf16[1,8,128,32]{2,3,1,0:T(8,128)(2,1)S(1)}, bf16[1,8,128,32]{2,3,1,0:T(8,128)(2,1)}, u32[]{:S(2)}) copy-start(bf16[1,8,128,32]{2,3,1,0:T(8,128)(2,1)} %get-tuple-element.143) | copy-start | bytes 196612
  101.4 8.6 %copy-start.27 = (bf16[1,8,128,32]{2,3,1,0:T(8,128)(2,1)S(1)}, bf16[1,8,128,32]{2,3,1,0:T(8,128)(2,1)}, u32[]{:S(2)}) copy-start(bf16[1,8,128,32]{2,3,1,0:T(8,128)(2,1)} %get-tuple-element.156) | copy-start | bytes 196612
  124.4 6.6 %copy-start.35 = (f32[64,16,2]{0,1,2:T(8,128)S(1)}, f32[64,16,2]{0,1,2:T(8,128)}, u32[]{:S(2)}) copy-start(f32[64,16,2]{0,1,2:T(8,128)} %add_reduce_fusion.11) | copy-start | bytes 24580
  132.6 7.0 %copy-start.8 = (f32[512,1,128]{2,0,1:T(8,128)}, f32[512,1,128]{2,0,1:T(8,128)S(1)}, u32[]{:S(2)}) copy-start(f32[512,1,128]{2,0,1:T(8,128)S(1)} %add_dynamic-update-slice_fusion.1) | copy-start | bytes 786436
  139.6 109.7 %all-reduce.10.cloned.1.call-start = ((), (), s32[]{:S(2)}) async-start(), calls=%async_computation | async-start | bytes 1572864 | tf_op jit(solution)/shard_map/psum | solution.py:240
  140.4 110.1 %copy-start.43 = (f32[128]{0:T(128)}, f32[128]{0:T(128)S(1)}, u32[]{:S(2)}) copy-start(f32[128]{0:T(128)S(1)} %tile.32) | copy-start | bytes 1540
  172.5 80.0 %copy-start.37 = (f32[3]{0:T(128)}, f32[3]{0:T(128)S(1)}, u32[]{:S(2)}) copy-start(f32[3]{0:T(128)S(1)} %fusion.51) | copy-start | bytes 40
  173.6 226.6 %all-reduce.16.cloned.1.call-start = ((), (), s32[]{:S(2)}) async-start(), calls=%async_computation.3 | async-start | bytes 655360 | tf_op jit(solution)/shard_map/psum | solution.py:260
  214.2 44.8 %copy-start.40 = (f32[16,2,2]{0,2,1:T(2,128)S(1)}, f32[16,2,2]{0,2,1:T(2,128)}, u32[]{:S(2)}) copy-start(f32[16,2,2]{0,2,1:T(2,128)} %copy-done.39) | copy-start | bytes 772
  214.2 44.8 %copy-start.42 = (f32[16,2,2]{0,2,1:T(2,128)S(1)}, f32[16,2,2]{0,2,1:T(2,128)}, u32[]{:S(2)}) copy-start(f32[16,2,2]{0,2,1:T(2,128)} %copy-done.41) | copy-start | bytes 772
  252.5 0.7 copy-start.6
  289.2 6.4 %copy-start.13 = (bf16[1,8,128,32]{2,3,1,0:T(8,128)(2,1)S(1)}, bf16[1,8,128,32]{2,3,1,0:T(8,128)(2,1)}, u32[]{:S(2)}) copy-start(bf16[1,8,128,32]{2,3,1,0:T(8,128)(2,1)} %get-tuple-element.133) | copy-start | bytes 196612
  289.2 6.5 %copy-start.14 = (bf16[1,8,128,32]{2,3,1,0:T(8,128)(2,1)S(1)}, bf16[1,8,128,32]{2,3,1,0:T(8,128)(2,1)}, u32[]{:S(2)}) copy-start(bf16[1,8,128,32]{2,3,1,0:T(8,128)(2,1)} %add_convert_fusion.1) | copy-start | bytes 196612
  296.1 0.8 copy-start.4
  308.0 2.8 copy-start.28
  308.0 2.8 copy-start.29
  323.6 1.5 copy-start.36
  324.3 4.0 copy-start.10
  324.3 4.0 copy-start.38
  326.1 1.5 copy-start.9
  326.1 111.9 %copy-start.7 = (f32[512,1,128]{2,0,1:T(8,128)S(1)}, f32[512,1,128]{2,0,1:T(8,128)}, u32[]{:S(2)}) copy-start(f32[512,1,128]{2,0,1:T(8,128)} %copy-done.6) | copy-start | bytes 786436
  326.1 111.9 %copy-start.44 = (f32[128]{0:T(128)S(1)}, f32[128]{0:T(128)}, u32[]{:S(2)}) copy-start(f32[128]{0:T(128)} %copy-done.43) | copy-start | bytes 1540
  326.1 111.9 %copy-start.45 = (f32[128]{0:T(128)S(1)}, f32[128]{0:T(128)}, u32[]{:S(2)}) copy-start(f32[128]{0:T(128)} %broadcast_multiply_fusion.4) | copy-start | bytes 1540
  328.2 108.5 %all-reduce.12.cloned.1.call-start = ((), (), s32[]{:S(2)}) async-start(), calls=%async_computation.1 | async-start | bytes 1572864 | tf_op jit(solution)/shard_map/psum | solution.py:240
  329.3 146.0 %all-reduce.14.cloned.1.call-start = ((), (), s32[]{:S(2)}) async-start(), calls=%async_computation.2 | async-start | bytes 1572864 | tf_op jit(solution)/shard_map/psum | solution.py:240
  (3 other events, 1.8 us)
Sparse Core Ops, SparseCore 0:
  139.7 72.8 all-reduce.17
  215.0 34.1 all-reduce.9
  328.3 71.8 all-reduce.15
  402.4 34.2 all-reduce.11
  440.3 35.0 all-reduce.13
where the time goes:
time: 491 us; the launch traced here: 486 us
  waiting for transfers between devices  213 us (43%)
  local copies, waits for them, and re-layouts  108 us (22%)
  other arithmetic  72.6 us (15%)
  blocking collectives  63.7 us (13%)
  between operations  18.6 us (4%)
  matrix products  9.01 us (2%)
    psum x2, waiting for transfers between devices, per_device(): gradient, curvature = lax.psum((grad_full, curv_full), 'pair')  109 us
    psum x3, waiting for transfers between devices, every_consensus(): lax.psum(project(current + dual_now / penalty_full, poly_basis), 'chan')  104 us
    all_gather x1, blocking collectives, per_device(): lax.all_gather(jones_init, 'pair', axis=0, tiled=True)  32.8 us
    all_gather x1, blocking collectives, per_device(): lax.all_gather(dual_init, 'pair', axis=0, tiled=True)  31 us
    mul x20, local copies, waits for them, and re-layouts, rotate_flat(): out_re = cosines * part_re - sines * part_im  30.3 us
    reduce_sum x4, other arithmetic, unrotate(): grad_re = -jnp.sum(neg_re * cosines + neg_im * sines, axis=1)  27.1 us
  transfers between devices with their start and end apart: 5, of which 5 were waited for; matrix products, arithmetic and copies ran while one was open for 2% of the time, Pallas kernels for 0%

commit v1 on v0

--- a/solution.py
+++ b/solution.py
@@ -2,6 +2,8 @@
 import jax.numpy as jnp
 import numpy as np
 from jax import lax
+from jax.experimental import pallas as pl
+from jax.experimental.pallas import tpu as pltpu
 from jax.sharding import PartitionSpec as P
 
 STATIONS = 512
@@ -270,6 +272,431 @@
     )
 
 
+AUX = 8
+
+
+def fused_kernel(
+    dims, basis, pid_ref, cnt_ref, flag_ref, jones_ref, dual_ref, rho_ref, sky_ref, vis_ref, theta_ref,
+    jones_out, dual_out, cons_out,
+    jfull, dfull, vzero, vone, vtwo, terms, trig, cosr, sinr, cosc, sinc, visp, fac,
+    jsend, jrecv, dsend, drecv, csend, crecv, vsend, vrecv,
+):
+    n, chans, outer, inner, rows, block, slots, dirs, poly, blocks = dims
+    width = 8 * dirs
+    part = block + AUX
+    f32, bf16 = jnp.float32, jnp.bfloat16
+    me = lax.axis_index("pair")
+    mc = lax.axis_index("chan")
+    mo, mi = me // inner, me % inner
+    out_peers = [lax.rem(mo + d, outer) * inner + mi for d in range(1, outer)]
+    in_peers = [mo * inner + lax.rem(mi + d, inner) for d in range(1, inner)]
+    chan_peers = [lax.rem(mc + d, chans) for d in range(1, chans)]
+
+    barrier = pltpu.get_barrier_semaphore()
+    for peer in out_peers + in_peers:
+        pl.semaphore_signal(barrier, inc=1, device_id={"pair": peer}, device_id_type=pl.DeviceIdType.MESH)
+    for peer in chan_peers:
+        pl.semaphore_signal(barrier, inc=1, device_id={"chan": peer}, device_id_type=pl.DeviceIdType.MESH)
+    pl.semaphore_wait(barrier, len(out_peers) + len(in_peers) + len(chan_peers))
+
+    pending = []
+
+    def push(source, target, ssem, rsem, where):
+        copy = pltpu.make_async_remote_copy(
+            src_ref=source, dst_ref=target, send_sem=ssem, recv_sem=rsem,
+            device_id=where, device_id_type=pl.DeviceIdType.MESH,
+        )
+        copy.start()
+        pending.append(copy)
+
+    def await_from(target, ssem, rsem, where):
+        pltpu.make_async_remote_copy(
+            src_ref=target, dst_ref=target, send_sem=ssem, recv_sem=rsem,
+            device_id=where, device_id_type=pl.DeviceIdType.MESH,
+        ).wait_recv()
+
+    def spread(source, slot_of, ssems, rsems):
+        for d, peer in enumerate(out_peers):
+            push(source, slot_of(me), ssems.at[d], rsems.at[me], {"pair": peer})
+        for d, peer in enumerate(in_peers):
+            push(source, slot_of(me), ssems.at[outer - 1 + d], rsems.at[me], {"pair": peer})
+
+    def relay(slot_of, ssems, rsems):
+        position = outer - 1 + inner - 1
+        for origin in out_peers:
+            await_from(slot_of(origin), ssems.at[0], rsems.at[origin], {"pair": origin})
+            for peer in in_peers:
+                push(slot_of(origin), slot_of(origin), ssems.at[position], rsems.at[origin], {"pair": peer})
+                position += 1
+
+    def finish(slot_of, ssems, rsems):
+        for peer in in_peers:
+            for step in range(outer):
+                origin = lax.rem(mo + step, outer) * inner + lax.rem(peer, inner)
+                await_from(slot_of(origin), ssems.at[0], rsems.at[origin], {"pair": peer})
+
+    def jslot(origin):
+        return jfull.at[pl.ds(pl.multiple_of(origin * rows, rows), rows)]
+
+    def dslot(origin):
+        return dfull.at[pl.ds(pl.multiple_of(origin * rows, rows), rows)]
+
+    spread(jones_ref, jslot, jsend, jrecv)
+    spread(dual_ref, dslot, dsend, drecv)
+    own_start = pl.multiple_of(me * rows, rows)
+    jfull[pl.ds(own_start, rows), :] = jones_ref[...]
+    dfull[pl.ds(own_start, rows), :] = dual_ref[...]
+
+    def chan_spread(buffer, first, count, level):
+        view = buffer.at[mc, pl.ds(first, count)]
+        for d, peer in enumerate(chan_peers):
+            push(view, view, vsend.at[level, d], vrecv.at[level, mc], {"chan": peer})
+
+    def chan_finish(buffer, first, count, level):
+        for peer in chan_peers:
+            await_from(
+                buffer.at[peer, pl.ds(first, count)], vsend.at[level, 0], vrecv.at[level, peer], {"chan": peer}
+            )
+
+    tile_k = lax.broadcasted_iota(jnp.int32, (dirs, width), 1) % dirs
+    tiling = (tile_k == lax.broadcasted_iota(jnp.int32, (dirs, width), 0)).astype(f32)
+
+    def widen(values):
+        return jnp.dot(values, tiling, precision=FULL_PRECISION, preferred_element_type=f32)
+
+    rho = widen(rho_ref[...])
+    sky = widen(sky_ref[...])
+    lane = lax.broadcasted_iota(jnp.int32, (1, width), 1)
+    imag_lane = (lane // (4 * dirs)) % 2 == 1
+    second_i = (lane // (2 * dirs)) % 2 == 1
+    second_j = (lane // dirs) % 2 == 1
+    sky_same = jnp.where(second_j, sky[1:2], sky[0:1])
+    sky_cross = sky[2:3]
+    sky_turn = jnp.where(second_j == imag_lane, sky[3:4], -sky[3:4])
+
+    def swap(values, second, gap):
+        return jnp.where(second, pltpu.roll(values, gap, 1), pltpu.roll(values, width - gap, 1))
+
+    def swap_c(values):
+        return pltpu.roll(values, 4 * dirs, 1)
+
+    def turn(values):
+        swapped = swap_c(values)
+        return jnp.where(imag_lane, swapped, -swapped)
+
+    def swap_i(values):
+        return swap(values, second_i, 2 * dirs)
+
+    def with_sky(values):
+        crossed = swap(values, second_j, dirs)
+        return values * sky_same + crossed * sky_cross + swap_c(crossed) * sky_turn
+
+    def both_rows(values):
+        swapped = swap_i(values)
+        return jnp.concatenate(
+            [jnp.where(second_i, swapped, values), jnp.where(second_i, values, swapped)], 0
+        )
+
+    def power(values):
+        squared = values * values
+        squared = squared + swap_c(squared)
+        return squared + swap_i(squared)
+
+    own_jones = jones_ref[...]
+    own_dual = dual_ref[...]
+    vzero[mc, pl.ds(0, rows), :] = own_jones + own_dual / rho
+    chan_spread(vzero, 0, rows, 0)
+
+    ratio = 1.0 + mc.astype(f32) / chans
+    trig_k = lax.broadcasted_iota(jnp.int32, (2 * dirs, 2 * width), 1)
+    trig_row = lax.broadcasted_iota(jnp.int32, (2 * dirs, 2 * width), 0)
+    trig_tiling = ((trig_k // width) * dirs + trig_k % dirs == trig_row).astype(f32)
+    for side, (cos_ref, sin_ref) in enumerate(((cosr, sinr), (cosc, sinc))):
+        angle = theta_ref[:, side, :] * ratio
+        cosines, sines = jnp.cos(angle), jnp.sin(angle)
+        for k in range(dirs):
+            trig[side, :, k, :] = cosines[:, k * block : (k + 1) * block]
+            trig[side, :, dirs + k, :] = sines[:, k * block : (k + 1) * block]
+
+        @pl.loop(0, slots)
+        def expand_slot(s):
+            wide = lax.dot_general(
+                trig[side, s], trig_tiling, (((0,), (0,)), ((), ())),
+                precision=FULL_PRECISION, preferred_element_type=f32,
+            )
+            cos_ref[s] = wide[:, :width]
+            sin_ref[s] = wide[:, width:]
+
+    relay(jslot, jsend, jrecv)
+
+    two = 2 * block
+    perm_row = lax.broadcasted_iota(jnp.int32, (two, two), 0)
+    perm_col = lax.broadcasted_iota(jnp.int32, (two, two), 1)
+    unlace = ((perm_row % block) * 2 + perm_row // block == perm_col).astype(f32).astype(bf16)
+    lace = ((perm_col % block) * 2 + perm_col // block == perm_row).astype(f32).astype(bf16)
+
+    @pl.loop(0, slots)
+    def unlace_slot(s):
+        for c in range(2):
+            half = jnp.dot(unlace, vis_ref[2 * s + c], preferred_element_type=f32).astype(bf16)
+            visp[s, :, c * two : (c + 1) * two] = jnp.dot(half, lace, preferred_element_type=f32).astype(bf16)
+
+    pid = pid_ref[0]
+    row_block = jnp.int32(0)
+    row_first = jnp.int32(0)
+    first = 0
+    for r in range(1, blocks):
+        first += blocks - r + 1
+        row_block = jnp.where(pid >= first, r, row_block)
+        row_first = jnp.where(pid >= first, first, row_first)
+    col_block = row_block + pid - row_first
+    apart = jnp.where(row_block == col_block, 0.0, 1.0).astype(f32)
+    samples = jnp.float32(0.0)
+    for s in range(slots):
+        samples = samples + jnp.where(s < cnt_ref[0], flag_ref[0, s], 0).astype(f32)
+
+    def load_block(buffer, which):
+        wanted = jnp.full((block, width), which, jnp.int32)
+        chosen = jnp.zeros((block, width), f32)
+        for b in range(blocks):
+            chosen = jnp.where(wanted == b, buffer[b * block : (b + 1) * block, :], chosen)
+        return chosen
+
+    upper = (lax.broadcasted_iota(jnp.int32, (two, 2 * two), 0) % block) < (
+        lax.broadcasted_iota(jnp.int32, (two, 2 * two), 1) % block
+    )
+    half_row = lax.broadcasted_iota(jnp.int32, (two, width), 0) // block == 1
+    wide_i = (lax.broadcasted_iota(jnp.int32, (two, width), 1) // (2 * dirs)) % 2 == 1
+    keep_left = half_row == wide_i
+    aux_row = lax.broadcasted_iota(jnp.int32, (AUX, width), 0)
+
+    def data_terms_here(level, row_jones, col_jones):
+        row_sky, col_sky = with_sky(row_jones), with_sky(col_jones)
+        for spot, source in enumerate((row_sky, col_jones, col_sky)):
+            fac[2 * spot] = both_rows(source)
+            fac[2 * spot + 1] = both_rows(turn(source))
+        row_total = samples * jnp.sum(power(row_sky), axis=0, keepdims=True)
+        col_total = samples * jnp.sum(power(col_sky), axis=0, keepdims=True)
+        row_id = row_block.astype(f32)
+        col_id = col_block.astype(f32)
+        same = samples * (1.0 - apart)
+        aux_r = jnp.where(aux_row == 0, col_total, jnp.where(aux_row == 1, same, row_id))
+        aux_c = jnp.where(aux_row == 0, row_total * apart, jnp.where(aux_row == 1, 0.0, col_id))
+
+        def slot_step(s, carry):
+            row_sum, col_sum = carry
+            weight = jnp.where(s < cnt_ref[0], flag_ref[0, s], 0).astype(f32)
+            weighting = jnp.where(upper, weight, weight * apart)
+            cos_r, sin_r = cosr[s], sinr[s]
+            cos_c, sin_c = cosc[s], sinc[s]
+            wide = [jnp.concatenate([x, x], 0) for x in (cos_r, sin_r, cos_c, sin_c)]
+
+            def rotated(spot, cosines, sines):
+                plain, turned = fac[2 * spot], fac[2 * spot + 1]
+                return (
+                    cosines * plain + sines * turned,
+                    cosines * turned - sines * plain,
+                )
+
+            left, left_turn = rotated(0, wide[0], wide[1])
+            conj, conj_turn = rotated(1, wide[2], wide[3])
+            right, right_turn = rotated(2, wide[2], wide[3])
+            left_only = jnp.where(keep_left, left, 0.0).astype(bf16)
+            model_rhs = jnp.concatenate([conj.astype(bf16), conj_turn.astype(bf16)], 0)
+            predicted = lax.dot_general(
+                left_only, model_rhs, (((1,), (1,)), ((), ())), preferred_element_type=f32
+            )
+            residual = (weighting * (visp[s].astype(f32) - predicted)).astype(bf16)
+            row_rhs = jnp.concatenate([right.astype(bf16), right_turn.astype(bf16)], 0)
+            row_out = jnp.dot(residual, row_rhs, preferred_element_type=f32)
+            col_out = lax.dot_general(
+                residual[:, :two], left.astype(bf16), (((0,), (0,)), ((), ())), preferred_element_type=f32
+            ) - lax.dot_general(
+                residual[:, two:], left_turn.astype(bf16), (((0,), (0,)), ((), ())), preferred_element_type=f32
+            )
+            row_pick = jnp.where(second_i, row_out[block:], row_out[:block])
+            col_pick = jnp.where(second_i, col_out[block:], col_out[:block])
+            row_sum = row_sum + (sin_r * turn(row_pick) - cos_r * row_pick)
+            col_sum = col_sum + (sin_c * turn(col_pick) - cos_c * col_pick)
+            return (row_sum, col_sum)
+
+        zero = jnp.zeros((block, width), f32)
+        row_grad, col_grad = lax.fori_loop(0, slots, slot_step, (zero, zero), unroll=UNROLL)
+        terms[level, me, pl.ds(0, block), :] = row_grad
+        terms[level, me, pl.ds(block, AUX), :] = aux_r
+        terms[level, me, pl.ds(part, block), :] = col_grad
+        terms[level, me, pl.ds(part + block, AUX), :] = aux_c
+
+    def term_slot(level):
+        return lambda origin: terms.at[level, origin]
+
+    def gathered(level, block_id, offset, count, jones_here):
+        wanted = block_id.astype(f32)
+        grad = jnp.zeros((count, width), f32)
+        shared = jnp.zeros((1, width), f32)
+        alone = jnp.zeros((1, width), f32)
+        for t in range(n):
+            for side in range(2):
+                base = side * part
+                aux = terms[level, t, pl.ds(base + block, AUX), :]
+                hit = aux[2:3] == wanted
+                grad = grad + jnp.where(hit, terms[level, t, pl.ds(base + offset, count), :], 0.0)
+                shared = shared + jnp.where(hit, aux[0:1], 0.0)
+                alone = alone + jnp.where(hit, aux[1:2], 0.0)
+        return grad, shared - alone * power(with_sky(jones_here))
+
+    def center_of(buffer, first, count):
+        values = [buffer[f, pl.ds(first, count), :] for f in range(chans)]
+        return [sum(float(basis[f, m]) * values[f] for f in range(chans)) for m in range(poly)]
+
+    mine = []
+    for m in range(poly):
+        coefficient = jnp.float32(basis[0, m])
+        for f in range(1, chans):
+            coefficient = jnp.where(mc == f, jnp.float32(basis[f, m]), coefficient)
+        mine.append(coefficient)
+
+    def expand_mine(center):
+        return sum(mine[m] * center[m] for m in range(poly))
+
+    def step_of(jones_here, duals_here, terms_here, target):
+        gradient, curvature = terms_here
+        return jones_here - STEP_SCALE * (
+            gradient + 0.5 * rho * (jones_here - target) + 0.5 * duals_here
+        ) / (curvature + 0.5 * rho)
+
+    finish(jslot, jsend, jrecv)
+    relay(dslot, dsend, drecv)
+    row_jones = load_block(jfull, row_block)
+    col_jones = load_block(jfull, col_block)
+    data_terms_here(0, row_jones, col_jones)
+    spread(terms.at[0, me], term_slot(0), csend.at[0], crecv.at[0])
+    finish(dslot, dsend, drecv)
+    row_dual = load_block(dfull, row_block)
+    col_dual = load_block(dfull, col_block)
+    vzero[mc, pl.ds(rows, block), :] = row_jones + row_dual / rho
+    vzero[mc, pl.ds(rows + block, block), :] = col_jones + col_dual / rho
+    chan_spread(vzero, rows, two, 1)
+    chan_finish(vzero, 0, rows, 0)
+    own_target = expand_mine(center_of(vzero, 0, rows))
+    relay(term_slot(0), csend.at[0], crecv.at[0])
+    chan_finish(vzero, rows, two, 1)
+    row_target = expand_mine(center_of(vzero, rows, block))
+    col_target = expand_mine(center_of(vzero, rows + block, block))
+    finish(term_slot(0), csend.at[0], crecv.at[0])
+
+    own_block = (me * rows) // block
+    own_offset = pl.multiple_of((me * rows) % block, AUX)
+    row_next = step_of(row_jones, row_dual, gathered(0, row_block, 0, block, row_jones), row_target)
+    col_next = step_of(col_jones, col_dual, gathered(0, col_block, 0, block, col_jones), col_target)
+    own_jones = step_of(
+        own_jones, own_dual, gathered(0, own_block, own_offset, rows, own_jones), own_target
+    )
+    vone[mc] = own_jones + own_dual / rho
+    chan_spread(vone, 0, rows, 2)
+    data_terms_here(1, row_next, col_next)
+    spread(terms.at[1, me], term_slot(1), csend.at[1], crecv.at[1])
+    chan_finish(vone, 0, rows, 2)
+    own_target = expand_mine(center_of(vone, 0, rows))
+    own_dual = own_dual + rho * (own_jones - own_target)
+    relay(term_slot(1), csend.at[1], crecv.at[1])
+    finish(term_slot(1), csend.at[1], crecv.at[1])
+    own_jones = step_of(
+        own_jones, own_dual, gathered(1, own_block, own_offset, rows, own_jones), own_target
+    )
+    vtwo[mc] = own_jones + own_dual / rho
+    chan_spread(vtwo, 0, rows, 3)
+    jones_out[...] = own_jones
+    chan_finish(vtwo, 0, rows, 3)
+    center = center_of(vtwo, 0, rows)
+    dual_out[...] = own_dual + rho * (own_jones - expand_mine(center))
+    for m in range(poly):
+        cons_out[:, m, :] = center[m]
+    for copy in pending:
+        copy.wait_send()
+
+
+UNROLL = 2
+
+
+def basis_table(chan_total):
+    middle = np.arange(chan_total, dtype=np.float64) + 0.5
+    degree = np.arange(NPOLY, dtype=np.float64)
+    normalizer = np.sqrt(np.where(degree == 0, 1.0, 2.0) / chan_total)
+    table = np.cos(np.pi * middle[:, None] * degree[None, :] / chan_total) * normalizer[None, :]
+    return table.astype(np.float32)
+
+
+def fused_device(
+    jones_init, dual_init, penalty, sky_flux, visibility, phases, pair_ids, counts, slot_flags
+):
+    rows, chan_dev, width = jones_init.shape
+    n, chans = lax.axis_size("pair"), lax.axis_size("chan")
+    tiles, slots = visibility.shape[0], visibility.shape[2]
+    two = visibility.shape[-1]
+    block, dirs = two // 2, penalty.shape[0]
+    if tiles != 1 or chan_dev != 1 or width != 128 or rows > block or rows % AUX:
+        return per_device(
+            jones_init, dual_init, penalty, sky_flux, visibility, phases, pair_ids, counts, slot_flags
+        )
+    inner = 2 if n % 2 == 0 else 1
+    outer = n // inner
+    blocks = n * rows // block
+    dims = (n, chans, outer, inner, rows, block, slots, dirs, NPOLY, blocks)
+    sends = outer - 1 + inner - 1 + (outer - 1) * (inner - 1)
+    basis = basis_table(chans)
+    part = block + AUX
+    f32 = jnp.float32
+    vmem = pl.BlockSpec(memory_space=pltpu.VMEM)
+    smem = pl.BlockSpec(memory_space=pltpu.SMEM)
+    dma = pltpu.SemaphoreType.DMA
+
+    def body(*refs):
+        fused_kernel(dims, basis, *refs)
+
+    jones_last, duals_last, center = pl.pallas_call(
+        body,
+        out_shape=(
+            jax.ShapeDtypeStruct((rows, width), f32),
+            jax.ShapeDtypeStruct((rows, width), f32),
+            jax.ShapeDtypeStruct((rows, NPOLY, width), f32),
+        ),
+        in_specs=[smem] * 3 + [vmem] * 6,
+        out_specs=(vmem, vmem, vmem),
+        scratch_shapes=[
+            pltpu.VMEM((n * rows, width), f32),
+            pltpu.VMEM((n * rows, width), f32),
+            pltpu.VMEM((chans, rows + two, width), f32),
+            pltpu.VMEM((chans, rows, width), f32),
+            pltpu.VMEM((chans, rows, width), f32),
+            pltpu.VMEM((ITERS, n, 2 * part, width), f32),
+            pltpu.VMEM((2, slots, 2 * dirs, block), f32),
+            pltpu.VMEM((slots, block, width), f32),
+            pltpu.VMEM((slots, block, width), f32),
+            pltpu.VMEM((slots, block, width), f32),
+            pltpu.VMEM((slots, block, width), f32),
+            pltpu.VMEM((slots, two, 2 * two), jnp.bfloat16),
+            pltpu.VMEM((6, two, width), f32),
+            dma((sends,)), dma((n,)), dma((sends,)), dma((n,)),
+            dma((ITERS, sends)), dma((ITERS, n)), dma((4, chans)), dma((4, chans)),
+        ],
+        compiler_params=pltpu.CompilerParams(
+            collective_id=0, has_side_effects=True, vmem_limit_bytes=48 * 1024 * 1024
+        ),
+    )(
+        pair_ids,
+        counts,
+        slot_flags,
+        jones_init.reshape(rows, width),
+        dual_init.reshape(rows, width),
+        penalty.reshape(1, dirs),
+        sky_flux.reshape(sky_flux.shape[1], dirs),
+        visibility.reshape(2 * slots, two, two),
+        phases.reshape(slots, 2, phases.shape[-1]),
+    )
+    return (jones_last.reshape(rows, 1, width), duals_last.reshape(rows, 1, width), center)
+
+
 def solution(mesh):
     in_specs = (
         P("pair", "chan", None),
@@ -284,5 +711,5 @@
     )
     out_specs = (P("pair", "chan", None), P("pair", "chan", None), P("pair", None, None))
     return jax.shard_map(
-        per_device, mesh=mesh, in_specs=in_specs, out_specs=out_specs, check_vma=False
-    )
+        fused_device, mesh=mesh, in_specs=in_specs, out_specs=out_specs, check_vma=False
+    )

time: 491 us -> 54.3 us (0.11); the launches traced: 486 us -> 53.8 us
  waiting for transfers between devices: 213 us -> 0 us
  local copies, waits for them, and re-layouts: 108 us -> 5.94 us
  other arithmetic: 72.6 us -> 0 us
  blocking collectives: 63.7 us -> 0 us
  Pallas kernels: 0 us -> 45.9 us
  between operations: 18.6 us -> 1.96 us
  matrix products: 9.01 us -> 0 us
    psum x5 -> x0, waiting for transfers between devices: 213 us -> none  [the longest x2 109 us: per_device(): gradient, curvature = lax.psum((grad_full, curv_full), 'pair')]
    all_gather x2 -> x0, blocking collectives: 63.7 us -> none  [the longest x1 32.8 us: per_device(): lax.all_gather(jones_init, 'pair', axis=0, tiled=True)]
    pallas_call x0 -> x1, Pallas kernels: none -> 45.9 us  [fused_device(): pl.pallas_call(body, out_shape=(jax.ShapeDtypeStruct((rows, width), f32),...]
    reduce_sum x15 -> x0, other arithmetic: 38 us -> none  [the longest x4 27.1 us: unrotate(): grad_re = -jnp.sum(neg_re * cosines + neg_im * sines, axis=1)]
    mul x26 -> x0, local copies, waits for them, and re-layouts: 36.7 us -> none  [the longest x20 30.3 us: rotate_flat(): out_re = cosines * part_re - sines * part_im]
    dot_general x4 -> x0, local copies, waits for them, and re-layouts: 17.7 us -> none  [the longest x2 8.93 us: slot_terms(): jnp.einsum('ftcpq,ftcpk->ftqk', residual, col_rhs, preferred_element_type...]
    neg x13 -> x0, other arithmetic: 12.6 us -> none  [the longest x4 4.81 us: unrotate(): grad_im = -jnp.sum(neg_im * cosines - neg_re * sines, axis=1)]
    neg x8 -> x0, local copies, waits for them, and re-layouts: 11.5 us -> none  [the longest x4 6.08 us: unrotate(): grad_re = -jnp.sum(neg_re * cosines + neg_im * sines, axis=1)]
  transfers between devices with their start and end apart: 5 -> 0, of which waited for: 5 -> 0; matrix products, arithmetic and copies ran while one was open for 2% -> 0% of each run, Pallas kernels for 0% -> 0%
where the time goes in v1:
time: 54.3 us; the launch traced here: 53.8 us
  Pallas kernels  45.9 us (85%)
  local copies, waits for them, and re-layouts  5.94 us (11%)
  between operations  1.96 us (4%)
    pallas_call x1, Pallas kernels, fused_device(): pl.pallas_call(body, out_shape=(jax.ShapeDtypeStruct((rows, width), f32),...  45.9 us
    unnamed x17, local copies, waits for them, and re-layouts  5.94 us

profile of v1, /device:TPU:0, one launch (start us, length us, event | category | flops | bytes accessed | tf_op | source)
XLA Modules:
  0.0 53.8 jit_solution(2659440665038053548)
XLA Ops:
  1.9 0.0 copy-start.4
  1.9 0.0 copy-start.5
  1.9 0.0 copy-start.6
  2.0 0.7 %copy-done.4 = f32[1,4,16]{2,1,0:T(4,128)S(1)} copy-done((f32[1,4,16]{2,1,0:T(4,128)S(1)}, f32[1,4,16]{2,1,0:T(4,128)}, u32[]{:S(2)}) %copy-start.4) | copy-done | bytes 280
  2.6 0.0 copy-done.5
  2.6 0.0 copy-done.6
  2.6 0.0 copy-start
  2.6 1.0 %copy-done = bf16[1,1,8,2,128,128]{5,4,3,2,1,0:T(8,128)(2,1)S(1)} copy-done((bf16[1,1,8,2,128,128]{5,4,3,2,1,0:T(8,128)(2,1)S(1)}, bf16[1,1,8,2,128,128]{5,4,3,2,1,0:T(8,128)(2,1)}, u32[]{:S(2)}) %copy-start) | copy-done | bytes 524312
  3.7 0.0 copy-start.1
  3.7 0.8 %copy-done.1 = f32[1,8,2,1024]{3,2,1,0:T(2,128)S(1)} copy-done((f32[1,8,2,1024]{3,2,1,0:T(2,128)S(1)}, f32[1,8,2,1024]{3,2,1,0:T(2,128)}, u32[]{:S(2)}) %copy-start.1) | copy-done | bytes 65560
  4.5 0.0 copy-start.2
  4.5 0.8 %copy-done.2 = f32[64,1,128]{2,1,0:T(1,128)S(1)} copy-done((f32[64,1,128]{2,1,0:T(1,128)S(1)}, f32[64,1,128]{2,1,0:T(1,128)}, u32[]{:S(2)}) %copy-start.2) | copy-done | bytes 32792
  5.3 0.0 copy-start.3
  5.3 0.8 %copy-done.3 = f32[64,1,128]{2,1,0:T(1,128)S(1)} copy-done((f32[64,1,128]{2,1,0:T(1,128)S(1)}, f32[64,1,128]{2,1,0:T(1,128)}, u32[]{:S(2)}) %copy-start.3) | copy-done | bytes 32792
  6.0 45.9 %shard_map.112 = (f32[64,128]{1,0:T(8,128)S(1)}, f32[64,128]{1,0:T(8,128)S(1)}, f32[64,3,128]{2,1,0:T(4,128)S(1)}) custom-call(s32[1]{0:T(128)S(6)} %copy.17.refs_0_, s32[1]{0:T(128)S(6)} %copy.18.refs_1_, s32[1,8]{1,0:T(1,128)S(1)} %copy-done.5, f32[64,128]{1,0:T(8,128)S(1)} %bitcast.14, f32[64,128]{1,0:T(8,128)S(1)} %bitcast.15, f32[1,16]{1,0:T(1,128)S(1)} %bitcast.19, ...), custom_call_target="tpu_custom_call" | custom-call | tf_op jit(solution)/shard_map/pallas_call | solution.py:657
  51.9 0.6 %copy.14 = f32[64,3,128]{2,0,1:T(8,128)} copy(f32[64,3,128]{2,1,0:T(4,128)S(1)} %get-tuple-element.11) | data formatting | bytes 196608
  52.5 0.6 %copy.19 = f32[64,1,128]{2,1,0:T(1,128)} copy(f32[64,1,128]{2,1,0:T(1,128)S(1)} %bitcast.17) | data formatting | bytes 65536
  53.1 0.6 %copy.20 = f32[64,1,128]{2,1,0:T(1,128)} copy(f32[64,1,128]{2,1,0:T(1,128)S(1)} %bitcast.16) | data formatting | bytes 65536
Async XLA Ops:
  1.9 0.7 %copy-start.4 = (f32[1,4,16]{2,1,0:T(4,128)S(1)}, f32[1,4,16]{2,1,0:T(4,128)}, u32[]{:S(2)}) copy-start(f32[1,4,16]{2,1,0:T(4,128)} %param.12) | copy-start | bytes 772
  1.9 0.7 %copy-start.5 = (s32[1,8]{1,0:T(1,128)S(1)}, s32[1,8]{1,0:T(1,128)}, u32[]{:S(2)}) copy-start(s32[1,8]{1,0:T(1,128)} %refs_2_.1) | copy-start | bytes 100
  1.9 0.7 %copy-start.6 = (f32[16]{0:T(128)S(1)}, f32[16]{0:T(128)}, u32[]{:S(2)}) copy-start(f32[16]{0:T(128)} %param.11) | copy-start | bytes 196
  2.6 1.0 %copy-start = (bf16[1,1,8,2,128,128]{5,4,3,2,1,0:T(8,128)(2,1)S(1)}, bf16[1,1,8,2,128,128]{5,4,3,2,1,0:T(8,128)(2,1)}, u32[]{:S(2)}) copy-start(bf16[1,1,8,2,128,128]{5,4,3,2,1,0:T(8,128)(2,1)} %param.13) | copy-start | bytes 1572868
  3.7 0.8 %copy-start.1 = (f32[1,8,2,1024]{3,2,1,0:T(2,128)S(1)}, f32[1,8,2,1024]{3,2,1,0:T(2,128)}, u32[]{:S(2)}) copy-start(f32[1,8,2,1024]{3,2,1,0:T(2,128)} %param.14) | copy-start | bytes 196612
  4.5 0.8 %copy-start.2 = (f32[64,1,128]{2,1,0:T(1,128)S(1)}, f32[64,1,128]{2,1,0:T(1,128)}, u32[]{:S(2)}) copy-start(f32[64,1,128]{2,1,0:T(1,128)} %param.9) | copy-start | bytes 98308
  5.3 0.8 %copy-start.3 = (f32[64,1,128]{2,1,0:T(1,128)S(1)}, f32[64,1,128]{2,1,0:T(1,128)}, u32[]{:S(2)}) copy-start(f32[64,1,128]{2,1,0:T(1,128)} %param.10) | copy-start | bytes 98308

commit v2 on v1

--- a/solution.py
+++ b/solution.py
@@ -275,11 +275,20 @@
 AUX = 8
 
 
+def flipped(value, mask):
+    bit = 1
+    while bit <= mask:
+        if mask & bit:
+            value = value + bit * (1 - 2 * ((value // bit) % 2))
+        bit *= 2
+    return value
+
+
 def fused_kernel(
-    dims, basis, pid_ref, cnt_ref, flag_ref, jones_ref, dual_ref, rho_ref, sky_ref, vis_ref, theta_ref,
+    dims, basis, pid_ref, cnt_ref, flag_ref, jones_hbm, dual_hbm, rho_ref, sky_ref, vis_hbm, theta_hbm,
     jones_out, dual_out, cons_out,
-    jfull, dfull, vzero, vone, vtwo, terms, trig, cosr, sinr, cosc, sinc, visp, fac,
-    jsend, jrecv, dsend, drecv, csend, crecv, vsend, vrecv,
+    jfull, dfull, vzero, vone, vtwo, terms, last, trig, cosr, sinr, cosc, sinc, visp, fac,
+    vis_ref, theta_ref, sums, inbox, jsend, jrecv, dsend, drecv, csend, crecv, vsend, vrecv, rsend, rrecv, local,
 ):
     n, chans, outer, inner, rows, block, slots, dirs, poly, blocks = dims
     width = 8 * dirs
@@ -288,7 +297,11 @@
     me = lax.axis_index("pair")
     mc = lax.axis_index("chan")
     mo, mi = me // inner, me % inner
-    out_peers = [lax.rem(mo + d, outer) * inner + mi for d in range(1, outer)]
+    if outer & (outer - 1):
+        out_rows = [lax.rem(mo + d, outer) for d in range(1, outer)]
+    else:
+        out_rows = [flipped(mo, d) for d in range(1, outer)]
+    out_peers = [o * inner + mi for o in out_rows]
     in_peers = [mo * inner + lax.rem(mi + d, inner) for d in range(1, inner)]
     chan_peers = [lax.rem(mc + d, chans) for d in range(1, chans)]
 
@@ -297,6 +310,17 @@
         pl.semaphore_signal(barrier, inc=1, device_id={"pair": peer}, device_id_type=pl.DeviceIdType.MESH)
     for peer in chan_peers:
         pl.semaphore_signal(barrier, inc=1, device_id={"chan": peer}, device_id_type=pl.DeviceIdType.MESH)
+    own_start = pl.multiple_of(me * rows, rows)
+    own_jref = jfull.at[pl.ds(own_start, rows)]
+    own_dref = dfull.at[pl.ds(own_start, rows)]
+    fetches = [
+        pltpu.make_async_copy(jones_hbm, own_jref, local.at[0]),
+        pltpu.make_async_copy(theta_hbm, theta_ref, local.at[1]),
+        pltpu.make_async_copy(dual_hbm, own_dref, local.at[2]),
+        pltpu.make_async_copy(vis_hbm, vis_ref, local.at[3]),
+    ]
+    for fetch in fetches:
+        fetch.start()
     pl.semaphore_wait(barrier, len(out_peers) + len(in_peers) + len(chan_peers))
 
     pending = []
@@ -329,11 +353,15 @@
                 push(slot_of(origin), slot_of(origin), ssems.at[position], rsems.at[origin], {"pair": peer})
                 position += 1
 
+    def late_origins():
+        return [o * inner + lax.rem(peer, inner) for peer in in_peers for o in [mo] + out_rows]
+
+    def await_late(origin, slot_of, ssems, rsems):
+        await_from(slot_of(origin), ssems.at[0], rsems.at[origin], {"pair": in_peers[0]})
+
     def finish(slot_of, ssems, rsems):
-        for peer in in_peers:
-            for step in range(outer):
-                origin = lax.rem(mo + step, outer) * inner + lax.rem(peer, inner)
-                await_from(slot_of(origin), ssems.at[0], rsems.at[origin], {"pair": peer})
+        for origin in late_origins():
+            await_late(origin, slot_of, ssems, rsems)
 
     def jslot(origin):
         return jfull.at[pl.ds(pl.multiple_of(origin * rows, rows), rows)]
@@ -341,11 +369,8 @@
     def dslot(origin):
         return dfull.at[pl.ds(pl.multiple_of(origin * rows, rows), rows)]
 
-    spread(jones_ref, jslot, jsend, jrecv)
-    spread(dual_ref, dslot, dsend, drecv)
-    own_start = pl.multiple_of(me * rows, rows)
-    jfull[pl.ds(own_start, rows), :] = jones_ref[...]
-    dfull[pl.ds(own_start, rows), :] = dual_ref[...]
+    fetches[0].wait()
+    spread(own_jref, jslot, jsend, jrecv)
 
     def chan_spread(buffer, first, count, level):
         view = buffer.at[mc, pl.ds(first, count)]
@@ -402,15 +427,11 @@
         squared = squared + swap_c(squared)
         return squared + swap_i(squared)
 
-    own_jones = jones_ref[...]
-    own_dual = dual_ref[...]
-    vzero[mc, pl.ds(0, rows), :] = own_jones + own_dual / rho
-    chan_spread(vzero, 0, rows, 0)
-
     ratio = 1.0 + mc.astype(f32) / chans
-    trig_k = lax.broadcasted_iota(jnp.int32, (2 * dirs, 2 * width), 1)
-    trig_row = lax.broadcasted_iota(jnp.int32, (2 * dirs, 2 * width), 0)
-    trig_tiling = ((trig_k // width) * dirs + trig_k % dirs == trig_row).astype(f32)
+    trig_k = lax.broadcasted_iota(jnp.int32, (6 * dirs, 2 * width), 1)
+    trig_row = lax.broadcasted_iota(jnp.int32, (6 * dirs, 2 * width), 0) % (2 * dirs)
+    trig_tiling = ((trig_k // width) * dirs + trig_k % dirs == trig_row).astype(f32).astype(bf16)
+    fetches[1].wait()
     for side, (cos_ref, sin_ref) in enumerate(((cosr, sinr), (cosc, sinc))):
         angle = theta_ref[:, side, :] * ratio
         cosines, sines = jnp.cos(angle), jnp.sin(angle)
@@ -418,16 +439,29 @@
             trig[side, :, k, :] = cosines[:, k * block : (k + 1) * block]
             trig[side, :, dirs + k, :] = sines[:, k * block : (k + 1) * block]
 
-        @pl.loop(0, slots)
-        def expand_slot(s):
+        for s in range(slots):
+            exact = trig[side, s]
+            high = exact.astype(bf16)
+            rest = exact - high.astype(f32)
+            middle = rest.astype(bf16)
+            low = (rest - middle.astype(f32)).astype(bf16)
             wide = lax.dot_general(
-                trig[side, s], trig_tiling, (((0,), (0,)), ((), ())),
-                precision=FULL_PRECISION, preferred_element_type=f32,
+                jnp.concatenate([high, middle, low], 0), trig_tiling, (((0,), (0,)), ((), ())),
+                preferred_element_type=f32,
             )
             cos_ref[s] = wide[:, :width]
             sin_ref[s] = wide[:, width:]
 
-    relay(jslot, jsend, jrecv)
+        if side == 0:
+            relay(jslot, jsend, jrecv)
+
+    fetches[2].wait()
+    spread(own_dref, dslot, dsend, drecv)
+    own_jones = own_jref[...]
+    own_dual = own_dref[...]
+    vzero[mc, pl.ds(0, rows), :] = own_jones + own_dual / rho
+    chan_spread(vzero, 0, rows, 0)
+    fetches[3].wait()
 
     two = 2 * block
     perm_row = lax.broadcasted_iota(jnp.int32, (two, two), 0)
@@ -435,8 +469,7 @@
     unlace = ((perm_row % block) * 2 + perm_row // block == perm_col).astype(f32).astype(bf16)
     lace = ((perm_col % block) * 2 + perm_col // block == perm_row).astype(f32).astype(bf16)
 
-    @pl.loop(0, slots)
-    def unlace_slot(s):
+    for s in range(slots):
         for c in range(2):
             half = jnp.dot(unlace, vis_ref[2 * s + c], preferred_element_type=f32).astype(bf16)
             visp[s, :, c * two : (c + 1) * two] = jnp.dot(half, lace, preferred_element_type=f32).astype(bf16)
@@ -470,7 +503,7 @@
     keep_left = half_row == wide_i
     aux_row = lax.broadcasted_iota(jnp.int32, (AUX, width), 0)
 
-    def data_terms_here(level, row_jones, col_jones):
+    def data_terms_here(row_jones, col_jones):
         row_sky, col_sky = with_sky(row_jones), with_sky(col_jones)
         for spot, source in enumerate((row_sky, col_jones, col_sky)):
             fac[2 * spot] = both_rows(source)
@@ -522,27 +555,30 @@
 
         zero = jnp.zeros((block, width), f32)
         row_grad, col_grad = lax.fori_loop(0, slots, slot_step, (zero, zero), unroll=UNROLL)
-        terms[level, me, pl.ds(0, block), :] = row_grad
-        terms[level, me, pl.ds(block, AUX), :] = aux_r
-        terms[level, me, pl.ds(part, block), :] = col_grad
-        terms[level, me, pl.ds(part + block, AUX), :] = aux_c
-
-    def term_slot(level):
-        return lambda origin: terms.at[level, origin]
-
-    def gathered(level, block_id, offset, count, jones_here):
+        return row_grad, aux_r, col_grad, aux_c
+
+    def term_slot(origin):
+        return terms.at[origin]
+
+    def gather_start(count):
+        return (
+            jnp.zeros((count, width), f32), jnp.zeros((1, width), f32), jnp.zeros((1, width), f32)
+        )
+
+    def gather_add(so_far, origin, block_id, offset, count):
         wanted = block_id.astype(f32)
-        grad = jnp.zeros((count, width), f32)
-        shared = jnp.zeros((1, width), f32)
-        alone = jnp.zeros((1, width), f32)
-        for t in range(n):
-            for side in range(2):
-                base = side * part
-                aux = terms[level, t, pl.ds(base + block, AUX), :]
-                hit = aux[2:3] == wanted
-                grad = grad + jnp.where(hit, terms[level, t, pl.ds(base + offset, count), :], 0.0)
-                shared = shared + jnp.where(hit, aux[0:1], 0.0)
-                alone = alone + jnp.where(hit, aux[1:2], 0.0)
+        grad, shared, alone = so_far
+        for side in range(2):
+            base = side * part
+            aux = terms[origin, pl.ds(base + block, AUX), :]
+            hit = aux[2:3] == wanted
+            grad = grad + jnp.where(hit, terms[origin, pl.ds(base + offset, count), :], 0.0)
+            shared = shared + jnp.where(hit, aux[0:1], 0.0)
+            alone = alone + jnp.where(hit, aux[1:2], 0.0)
+        return grad, shared, alone
+
+    def gather_end(so_far, jones_here):
+        grad, shared, alone = so_far
         return grad, shared - alone * power(with_sky(jones_here))
 
     def center_of(buffer, first, count):
@@ -569,40 +605,100 @@
     relay(dslot, dsend, drecv)
     row_jones = load_block(jfull, row_block)
     col_jones = load_block(jfull, col_block)
-    data_terms_here(0, row_jones, col_jones)
-    spread(terms.at[0, me], term_slot(0), csend.at[0], crecv.at[0])
+    row_grad, aux_r, col_grad, aux_c = data_terms_here(row_jones, col_jones)
+    terms[me, pl.ds(0, block), :] = row_grad
+    terms[me, pl.ds(block, AUX), :] = aux_r
+    terms[me, pl.ds(part, block), :] = col_grad
+    terms[me, pl.ds(part + block, AUX), :] = aux_c
+    spread(terms.at[me], term_slot, csend, crecv)
     finish(dslot, dsend, drecv)
     row_dual = load_block(dfull, row_block)
     col_dual = load_block(dfull, col_block)
     vzero[mc, pl.ds(rows, block), :] = row_jones + row_dual / rho
     vzero[mc, pl.ds(rows + block, block), :] = col_jones + col_dual / rho
     chan_spread(vzero, rows, two, 1)
+    relay(term_slot, csend, crecv)
+    row_so = gather_start(block)
+    col_so = gather_start(block)
+    for origin in [me] + out_peers:
+        row_so = gather_add(row_so, origin, row_block, 0, block)
+        col_so = gather_add(col_so, origin, col_block, 0, block)
     chan_finish(vzero, 0, rows, 0)
+    chan_finish(vzero, rows, two, 1)
     own_target = expand_mine(center_of(vzero, 0, rows))
-    relay(term_slot(0), csend.at[0], crecv.at[0])
-    chan_finish(vzero, rows, two, 1)
     row_target = expand_mine(center_of(vzero, rows, block))
     col_target = expand_mine(center_of(vzero, rows + block, block))
-    finish(term_slot(0), csend.at[0], crecv.at[0])
+    for origin in late_origins():
+        await_late(origin, term_slot, csend, crecv)
+        row_so = gather_add(row_so, origin, row_block, 0, block)
+        col_so = gather_add(col_so, origin, col_block, 0, block)
+    row_next = step_of(row_jones, row_dual, gather_end(row_so, row_jones), row_target)
+    col_next = step_of(col_jones, col_dual, gather_end(col_so, col_jones), col_target)
+
+    row_grad, aux_r, col_grad, aux_c = data_terms_here(row_next, col_next)
+    last[pl.ds(0, block), :] = row_grad
+    last[pl.ds(block, block), :] = col_grad
+    message = rows + AUX
+
+    def meant_for(owner):
+        owner_block = (owner * rows) // block
+        offset = pl.multiple_of((owner * rows) % block, AUX)
+        to_row = jnp.where(jnp.full((1, width), row_block, jnp.int32) == owner_block, 1, 0) == 1
+        to_col = jnp.where(jnp.full((1, width), col_block, jnp.int32) == owner_block, 1, 0) == 1
+        grad = jnp.where(to_row, last[pl.ds(offset, rows), :], 0.0) + jnp.where(
+            to_col, last[pl.ds(block + offset, rows), :], 0.0
+        )
+        return grad, jnp.where(to_row, aux_r, 0.0) + jnp.where(to_col, aux_c, 0.0)
+
+    for d, peer in enumerate(in_peers):
+        far = lax.rem(peer, inner)
+        for z, o in enumerate(out_rows + [mo]):
+            spot = d * outer + z
+            grad, aux = meant_for(o * inner + far)
+            sums[spot, pl.ds(0, rows), :] = grad
+            sums[spot, pl.ds(rows, AUX), :] = aux
+            push(
+                sums.at[spot], inbox.at[mi * outer + o], rsend.at[spot], rrecv.at[mi * outer + o], {"pair": peer}
+            )
+    base = (inner - 1) * outer
+    arrivals = inner * outer
+    total = None
+    for z, o in enumerate(out_rows + [mo]):
+        grad, aux = meant_for(o * inner + mi)
+        for d, peer in enumerate(in_peers):
+            place = lax.rem(peer, inner) * outer + o
+            await_from(inbox.at[place], rsend.at[0], rrecv.at[place], {"pair": peer})
+            grad = grad + inbox[place, pl.ds(0, rows), :]
+            aux = aux + inbox[place, pl.ds(rows, AUX), :]
+        if z < outer - 1:
+            sums[base + z, pl.ds(0, rows), :] = grad
+            sums[base + z, pl.ds(rows, AUX), :] = aux
+            push(
+                sums.at[base + z], inbox.at[arrivals + mo], rsend.at[base + z], rrecv.at[arrivals + mo],
+                {"pair": o * inner + mi},
+            )
+        else:
+            total = (grad, aux)
 
     own_block = (me * rows) // block
     own_offset = pl.multiple_of((me * rows) % block, AUX)
-    row_next = step_of(row_jones, row_dual, gathered(0, row_block, 0, block, row_jones), row_target)
-    col_next = step_of(col_jones, col_dual, gathered(0, col_block, 0, block, col_jones), col_target)
-    own_jones = step_of(
-        own_jones, own_dual, gathered(0, own_block, own_offset, rows, own_jones), own_target
-    )
+    own_so = gather_start(rows)
+    for origin in [me] + out_peers + late_origins():
+        own_so = gather_add(own_so, origin, own_block, own_offset, rows)
+    own_jones = step_of(own_jones, own_dual, gather_end(own_so, own_jones), own_target)
     vone[mc] = own_jones + own_dual / rho
     chan_spread(vone, 0, rows, 2)
-    data_terms_here(1, row_next, col_next)
-    spread(terms.at[1, me], term_slot(1), csend.at[1], crecv.at[1])
     chan_finish(vone, 0, rows, 2)
     own_target = expand_mine(center_of(vone, 0, rows))
     own_dual = own_dual + rho * (own_jones - own_target)
-    relay(term_slot(1), csend.at[1], crecv.at[1])
-    finish(term_slot(1), csend.at[1], crecv.at[1])
+    grad, aux = total
+    for z, o in enumerate(out_rows):
+        place = arrivals + o
+        await_from(inbox.at[place], rsend.at[0], rrecv.at[place], {"pair": out_peers[z]})
+        grad = grad + inbox[place, pl.ds(0, rows), :]
+        aux = aux + inbox[place, pl.ds(rows, AUX), :]
     own_jones = step_of(
-        own_jones, own_dual, gathered(1, own_block, own_offset, rows, own_jones), own_target
+        own_jones, own_dual, gather_end((grad, aux[0:1], aux[1:2]), own_jones), own_target
     )
     vtwo[mc] = own_jones + own_dual / rho
     chan_spread(vtwo, 0, rows, 3)
@@ -616,7 +712,7 @@
         copy.wait_send()
 
 
-UNROLL = 2
+UNROLL = 4
 
 
 def basis_table(chan_total):
@@ -648,6 +744,7 @@
     part = block + AUX
     f32 = jnp.float32
     vmem = pl.BlockSpec(memory_space=pltpu.VMEM)
+    hbm = pl.BlockSpec(memory_space=pltpu.HBM)
     smem = pl.BlockSpec(memory_space=pltpu.SMEM)
     dma = pltpu.SemaphoreType.DMA
 
@@ -661,7 +758,7 @@
             jax.ShapeDtypeStruct((rows, width), f32),
             jax.ShapeDtypeStruct((rows, NPOLY, width), f32),
         ),
-        in_specs=[smem] * 3 + [vmem] * 6,
+        in_specs=[smem] * 3 + [hbm] * 2 + [vmem] * 2 + [hbm] * 2,
         out_specs=(vmem, vmem, vmem),
         scratch_shapes=[
             pltpu.VMEM((n * rows, width), f32),
@@ -669,7 +766,8 @@
             pltpu.VMEM((chans, rows + two, width), f32),
             pltpu.VMEM((chans, rows, width), f32),
             pltpu.VMEM((chans, rows, width), f32),
-            pltpu.VMEM((ITERS, n, 2 * part, width), f32),
+            pltpu.VMEM((n, 2 * part, width), f32),
+            pltpu.VMEM((two, width), f32),
             pltpu.VMEM((2, slots, 2 * dirs, block), f32),
             pltpu.VMEM((slots, block, width), f32),
             pltpu.VMEM((slots, block, width), f32),
@@ -677,8 +775,13 @@
             pltpu.VMEM((slots, block, width), f32),
             pltpu.VMEM((slots, two, 2 * two), jnp.bfloat16),
             pltpu.VMEM((6, two, width), f32),
+            pltpu.VMEM((2 * slots, two, two), jnp.bfloat16),
+            pltpu.VMEM((slots, 2, phases.shape[-1]), f32),
+            pltpu.VMEM((n, rows + AUX, width), f32),
+            pltpu.VMEM((n + outer, rows + AUX, width), f32),
             dma((sends,)), dma((n,)), dma((sends,)), dma((n,)),
-            dma((ITERS, sends)), dma((ITERS, n)), dma((4, chans)), dma((4, chans)),
+            dma((sends,)), dma((n,)), dma((4, chans)), dma((4, chans)),
+            dma((n,)), dma((n + outer,)), dma((4,)),
         ],
         compiler_params=pltpu.CompilerParams(
             collective_id=0, has_side_effects=True, vmem_limit_bytes=48 * 1024 * 1024

time: 54.3 us -> 50.6 us (0.932)
  Pallas kernels: 45.9 us -> 42.4 us
    pallas_call x1, Pallas kernels: 45.9 us -> 42.4 us  [fused_device(): pl.pallas_call(body, out_shape=(jax.ShapeDtypeStruct((rows, width), f32),...]
where the time goes in v2:
time: 50.6 us; the launch traced here: 50.3 us
  Pallas kernels  42.4 us (84%)
  local copies, waits for them, and re-layouts  5.94 us (12%)
  between operations  1.96 us (4%)
    pallas_call x1, Pallas kernels, fused_device(): pl.pallas_call(body, out_shape=(jax.ShapeDtypeStruct((rows, width), f32),...  42.4 us
    unnamed x17, local copies, waits for them, and re-layouts  5.94 us

profile of v2, /device:TPU:0, one launch (start us, length us, event | category | flops | bytes accessed | tf_op | source)
XLA Modules:
  0.0 50.3 jit_solution(11273406290305774111)
XLA Ops:
  1.9 0.0 copy-start.4
  1.9 0.0 copy-start.5
  1.9 0.0 copy-start.6
  2.0 0.7 %copy-done.4 = f32[1,4,16]{2,1,0:T(4,128)S(1)} copy-done((f32[1,4,16]{2,1,0:T(4,128)S(1)}, f32[1,4,16]{2,1,0:T(4,128)}, u32[]{:S(2)}) %copy-start.4) | copy-done | bytes 280
  2.6 0.0 copy-done.5
  2.6 0.0 copy-done.6
  2.6 0.0 copy-start
  2.6 1.0 %copy-done = bf16[1,1,8,2,128,128]{5,4,3,2,1,0:T(8,128)(2,1)S(1)} copy-done((bf16[1,1,8,2,128,128]{5,4,3,2,1,0:T(8,128)(2,1)S(1)}, bf16[1,1,8,2,128,128]{5,4,3,2,1,0:T(8,128)(2,1)}, u32[]{:S(2)}) %copy-start) | copy-done | bytes 524312
  3.7 0.0 copy-start.1
  3.7 0.8 %copy-done.1 = f32[1,8,2,1024]{3,2,1,0:T(2,128)S(1)} copy-done((f32[1,8,2,1024]{3,2,1,0:T(2,128)S(1)}, f32[1,8,2,1024]{3,2,1,0:T(2,128)}, u32[]{:S(2)}) %copy-start.1) | copy-done | bytes 65560
  4.5 0.0 copy-start.2
  4.5 0.8 %copy-done.2 = f32[64,1,128]{2,1,0:T(1,128)S(1)} copy-done((f32[64,1,128]{2,1,0:T(1,128)S(1)}, f32[64,1,128]{2,1,0:T(1,128)}, u32[]{:S(2)}) %copy-start.2) | copy-done | bytes 32792
  5.3 0.0 copy-start.3
  5.3 0.8 %copy-done.3 = f32[64,1,128]{2,1,0:T(1,128)S(1)} copy-done((f32[64,1,128]{2,1,0:T(1,128)S(1)}, f32[64,1,128]{2,1,0:T(1,128)}, u32[]{:S(2)}) %copy-start.3) | copy-done | bytes 32792
  6.0 42.4 %shard_map.112 = (f32[64,128]{1,0:T(8,128)S(1)}, f32[64,128]{1,0:T(8,128)S(1)}, f32[64,3,128]{2,1,0:T(4,128)S(1)}) custom-call(s32[1]{0:T(128)S(6)} %copy.17.refs_0_, s32[1]{0:T(128)S(6)} %copy.18.refs_1_, s32[1,8]{1,0:T(1,128)S(1)} %copy-done.5, f32[64,128]{1,0:T(8,128)S(1)} %bitcast.14, f32[64,128]{1,0:T(8,128)S(1)} %bitcast.15, f32[1,16]{1,0:T(1,128)S(1)} %bitcast.19, ...), custom_call_target="tpu_custom_call" | custom-call | tf_op jit(solution)/shard_map/pallas_call | solution.py:754
  48.4 0.6 %copy.14 = f32[64,3,128]{2,0,1:T(8,128)} copy(f32[64,3,128]{2,1,0:T(4,128)S(1)} %get-tuple-element.11) | data formatting | bytes 196608
  49.0 0.6 %copy.19 = f32[64,1,128]{2,1,0:T(1,128)} copy(f32[64,1,128]{2,1,0:T(1,128)S(1)} %bitcast.17) | data formatting | bytes 65536
  49.6 0.6 %copy.20 = f32[64,1,128]{2,1,0:T(1,128)} copy(f32[64,1,128]{2,1,0:T(1,128)S(1)} %bitcast.16) | data formatting | bytes 65536
Async XLA Ops:
  1.9 0.7 %copy-start.4 = (f32[1,4,16]{2,1,0:T(4,128)S(1)}, f32[1,4,16]{2,1,0:T(4,128)}, u32[]{:S(2)}) copy-start(f32[1,4,16]{2,1,0:T(4,128)} %param.12) | copy-start | bytes 772
  1.9 0.7 %copy-start.5 = (s32[1,8]{1,0:T(1,128)S(1)}, s32[1,8]{1,0:T(1,128)}, u32[]{:S(2)}) copy-start(s32[1,8]{1,0:T(1,128)} %refs_2_.1) | copy-start | bytes 100
  1.9 0.7 %copy-start.6 = (f32[16]{0:T(128)S(1)}, f32[16]{0:T(128)}, u32[]{:S(2)}) copy-start(f32[16]{0:T(128)} %param.11) | copy-start | bytes 196
  2.6 1.0 %copy-start = (bf16[1,1,8,2,128,128]{5,4,3,2,1,0:T(8,128)(2,1)S(1)}, bf16[1,1,8,2,128,128]{5,4,3,2,1,0:T(8,128)(2,1)}, u32[]{:S(2)}) copy-start(bf16[1,1,8,2,128,128]{5,4,3,2,1,0:T(8,128)(2,1)} %param.13) | copy-start | bytes 1572868
  3.7 0.8 %copy-start.1 = (f32[1,8,2,1024]{3,2,1,0:T(2,128)S(1)}, f32[1,8,2,1024]{3,2,1,0:T(2,128)}, u32[]{:S(2)}) copy-start(f32[1,8,2,1024]{3,2,1,0:T(2,128)} %param.14) | copy-start | bytes 196612
  4.5 0.8 %copy-start.2 = (f32[64,1,128]{2,1,0:T(1,128)S(1)}, f32[64,1,128]{2,1,0:T(1,128)}, u32[]{:S(2)}) copy-start(f32[64,1,128]{2,1,0:T(1,128)} %param.9) | copy-start | bytes 98308
  5.3 0.8 %copy-start.3 = (f32[64,1,128]{2,1,0:T(1,128)S(1)}, f32[64,1,128]{2,1,0:T(1,128)}, u32[]{:S(2)}) copy-start(f32[64,1,128]{2,1,0:T(1,128)} %param.10) | copy-start | bytes 98308

commit v3 on v2

--- a/solution.py
+++ b/solution.py
@@ -345,13 +345,19 @@
         for d, peer in enumerate(in_peers):
             push(source, slot_of(me), ssems.at[outer - 1 + d], rsems.at[me], {"pair": peer})
 
-    def relay(slot_of, ssems, rsems):
+    def relay_all(streams):
         position = outer - 1 + inner - 1
         for origin in out_peers:
-            await_from(slot_of(origin), ssems.at[0], rsems.at[origin], {"pair": origin})
-            for peer in in_peers:
-                push(slot_of(origin), slot_of(origin), ssems.at[position], rsems.at[origin], {"pair": peer})
-                position += 1
+            for slot_of, ssems, rsems in streams:
+                await_from(slot_of(origin), ssems.at[0], rsems.at[origin], {"pair": origin})
+                for d, peer in enumerate(in_peers):
+                    push(
+                        slot_of(origin), slot_of(origin), ssems.at[position + d], rsems.at[origin], {"pair": peer}
+                    )
+            position += inner - 1
+
+    def relay(slot_of, ssems, rsems):
+        relay_all([(slot_of, ssems, rsems)])
 
     def late_origins():
         return [o * inner + lax.rem(peer, inner) for peer in in_peers for o in [mo] + out_rows]
@@ -503,7 +509,7 @@
     keep_left = half_row == wide_i
     aux_row = lax.broadcasted_iota(jnp.int32, (AUX, width), 0)
 
-    def data_terms_here(row_jones, col_jones):
+    def data_terms_here(row_jones, col_jones, between=None):
         row_sky, col_sky = with_sky(row_jones), with_sky(col_jones)
         for spot, source in enumerate((row_sky, col_jones, col_sky)):
             fac[2 * spot] = both_rows(source)
@@ -554,11 +560,18 @@
             return (row_sum, col_sum)
 
         zero = jnp.zeros((block, width), f32)
-        row_grad, col_grad = lax.fori_loop(0, slots, slot_step, (zero, zero), unroll=UNROLL)
+        middle = slots // 2 if between else slots
+        sums_here = lax.fori_loop(0, middle, slot_step, (zero, zero), unroll=UNROLL)
+        if between:
+            between()
+            sums_here = lax.fori_loop(middle, slots, slot_step, sums_here, unroll=UNROLL)
+        row_grad, col_grad = sums_here
         return row_grad, aux_r, col_grad, aux_c
 
-    def term_slot(origin):
-        return terms.at[origin]
+    def term_half(side):
+        return lambda origin: terms.at[origin, pl.ds(side * part, part)]
+
+    term_streams = [(term_half(side), csend.at[side], crecv.at[side]) for side in range(2)]
 
     def gather_start(count):
         return (
@@ -602,22 +615,24 @@
         ) / (curvature + 0.5 * rho)
 
     finish(jslot, jsend, jrecv)
-    relay(dslot, dsend, drecv)
     row_jones = load_block(jfull, row_block)
     col_jones = load_block(jfull, col_block)
-    row_grad, aux_r, col_grad, aux_c = data_terms_here(row_jones, col_jones)
+    row_grad, aux_r, col_grad, aux_c = data_terms_here(
+        row_jones, col_jones, lambda: relay(dslot, dsend, drecv)
+    )
     terms[me, pl.ds(0, block), :] = row_grad
     terms[me, pl.ds(block, AUX), :] = aux_r
     terms[me, pl.ds(part, block), :] = col_grad
     terms[me, pl.ds(part + block, AUX), :] = aux_c
-    spread(terms.at[me], term_slot, csend, crecv)
+    for slot_of, ssems, rsems in term_streams:
+        spread(slot_of(me), slot_of, ssems, rsems)
     finish(dslot, dsend, drecv)
     row_dual = load_block(dfull, row_block)
     col_dual = load_block(dfull, col_block)
     vzero[mc, pl.ds(rows, block), :] = row_jones + row_dual / rho
     vzero[mc, pl.ds(rows + block, block), :] = col_jones + col_dual / rho
     chan_spread(vzero, rows, two, 1)
-    relay(term_slot, csend, crecv)
+    relay_all(term_streams)
     row_so = gather_start(block)
     col_so = gather_start(block)
     for origin in [me] + out_peers:
@@ -629,7 +644,8 @@
     row_target = expand_mine(center_of(vzero, rows, block))
     col_target = expand_mine(center_of(vzero, rows + block, block))
     for origin in late_origins():
-        await_late(origin, term_slot, csend, crecv)
+        for stream in term_streams:
+            await_late(origin, *stream)
         row_so = gather_add(row_so, origin, row_block, 0, block)
         col_so = gather_add(col_so, origin, col_block, 0, block)
     row_next = step_of(row_jones, row_dual, gather_end(row_so, row_jones), row_target)
@@ -780,11 +796,11 @@
             pltpu.VMEM((n, rows + AUX, width), f32),
             pltpu.VMEM((n + outer, rows + AUX, width), f32),
             dma((sends,)), dma((n,)), dma((sends,)), dma((n,)),
-            dma((sends,)), dma((n,)), dma((4, chans)), dma((4, chans)),
+            dma((2, sends)), dma((2, n)), dma((4, chans)), dma((4, chans)),
             dma((n,)), dma((n + outer,)), dma((4,)),
         ],
         compiler_params=pltpu.CompilerParams(
-            collective_id=0, has_side_effects=True, vmem_limit_bytes=48 * 1024 * 1024
+            collective_id=0, has_side_effects=True, vmem_limit_bytes=67043328
         ),
     )(
         pair_ids,

time: 50.6 us -> 47 us (0.929)
  local copies, waits for them, and re-layouts: 5.94 us -> 2.95 us
    unnamed x17 -> x7, local copies, waits for them, and re-layouts: 5.94 us -> 2.95 us
where the time goes in v3:
time: 47 us; the launch traced here: 46.8 us
  Pallas kernels  41.9 us (89%)
  local copies, waits for them, and re-layouts  2.95 us (6%)
  between operations  1.94 us (4%)
    pallas_call x1, Pallas kernels, fused_device(): pl.pallas_call(body, out_shape=(jax.ShapeDtypeStruct((rows, width), f32),...  41.9 us
    unnamed x7, local copies, waits for them, and re-layouts  2.95 us

profile of v3, /device:TPU:0, one launch (start us, length us, event | category | flops | bytes accessed | tf_op | source)
XLA Modules:
  0.0 46.8 jit_solution(11746620658807027033)
XLA Ops:
  1.9 41.9 %shard_map.112 = (f32[64,128]{1,0:T(8,128)}, f32[64,128]{1,0:T(8,128)}, f32[64,3,128]{2,1,0:T(4,128)}) custom-call(s32[1]{0:T(128)S(6)} %copy.17.refs_0_, s32[1]{0:T(128)S(6)} %copy.18.refs_1_, s32[1,8]{1,0:T(1,128)} %refs_2_.1, f32[64,128]{1,0:T(8,128)} %bitcast.14, f32[64,128]{1,0:T(8,128)} %bitcast.15, f32[1,16]{1,0:T(1,128)} %bitcast.19, ...), custom_call_target="tpu_custom_call" | custom-call | tf_op jit(solution)/shard_map/pallas_call | solution.py:770
  43.8 0.0 copy-start.1
  43.8 1.6 %copy.14 = f32[64,3,128]{2,0,1:T(8,128)} copy(f32[64,3,128]{2,1,0:T(4,128)} %get-tuple-element.11) | data formatting | bytes 196608
  45.4 0.0 copy-done.1
  45.4 0.0 copy-start
  45.4 0.6 %copy.19 = f32[64,1,128]{2,1,0:T(1,128)} copy(f32[64,1,128]{2,1,0:T(1,128)S(1)} %bitcast.17) | data formatting | bytes 65536
  46.0 0.2 copy-done
  46.2 0.6 %copy.20 = f32[64,1,128]{2,1,0:T(1,128)} copy(f32[64,1,128]{2,1,0:T(1,128)S(1)} %bitcast.16) | data formatting | bytes 65536
Async XLA Ops:
  43.8 1.6 %copy-start.1 = (f32[64,128]{1,0:T(8,128)S(1)}, f32[64,128]{1,0:T(8,128)}, u32[]{:S(2)}) copy-start(f32[64,128]{1,0:T(8,128)} %get-tuple-element.6) | copy-start | bytes 98308
  45.4 0.8 %copy-start = (f32[64,128]{1,0:T(8,128)S(1)}, f32[64,128]{1,0:T(8,128)}, u32[]{:S(2)}) copy-start(f32[64,128]{1,0:T(8,128)} %get-tuple-element.7) | copy-start | bytes 98308
